TPU v7x, 1024 devices: a whole 8x8x8 slice. The times are simulated.
1024 devices in a mesh: slab: 16 (over x, core), dom: 64 (over y, z).
Axes of the slice: x: 8, y: 8, z: 8, core: 2. Of those that a mesh axis runs over, the one named last changes fastest.
Arguments:
- coords: float32 [3, 16, 64, 512], P(None, 'slab', 'dom'), may hold values from -6 to 6
- velocity: float32 [3, 16, 64, 512], P(None, 'slab', 'dom'), may hold values from -6 to 6
- charge: float32 [16, 64, 512], P('slab', 'dom'), may hold values from -1 to 1
- inv_mass: float32 [16, 64, 512], P('slab', 'dom'), may hold values from 0.0625 to 1
- tile_block: int32 [16, 64, 64], P('slab', 'dom'), may hold values from 0 to 3
- tile_atoms: int32 [16, 64, 64, 128], P('slab', 'dom'), may hold values from 0 to 2047
- active_tile_count: int32 [16, 64], P('slab', 'dom'), may hold values from 1 to 64
- bond_atoms: int32 [2, 16, 64, 256], P(None, 'slab', 'dom'), may hold values from 0 to 511, as said below
- cross_atoms: int32 [2, 16, 64, 128], P(None, 'slab', 'dom'), may hold values from 0 to 255
- cross_side: int32 [16, 64, 128], P('slab', 'dom'), may hold values from 0 to 3
- cross_count: int32 [16, 64], P('slab', 'dom'), may hold values from 1 to 128
Outputs:
- coords_out: float32 [3, 16, 64, 512], P(None, 'slab', 'dom')
- velocity_out: float32 [3, 16, 64, 512], P(None, 'slab', 'dom')
Inputs may be any that keep to these rules, and one draw needn't show every extreme that they name: `bond_atoms`: each bond joins two different atoms of the domain that holds it. `cross_atoms`: row 0 is an atom of the owning domain, row 1 an atom of the neighbour named by cross_side; both are among the first 256 atoms of their domains. `cross_side`: codes 0 to 3 name the in-slab neighbours at offsets +1, -1, +8, -8 along dom, cyclically. `cross_count`: slots below the count are live. `active_tile_count`: tiles below the count are live. `tile_atoms`: entries index the domain's halo list as in the first step.
All inputs are finite; a program needn't handle non-finite values.
Results may differ from a plain program's by a relative error of at most 0.0003.
Values sent between devices are 32-bit elements; how exact they have to be, the bound alone decides.
A program may use at most 32 MiB of HBM per device.

v0:
```python
import jax
import jax.numpy as jnp
from jax import lax
from jax.sharding import PartitionSpec as P

TILE = 128
ORDER = 4


time_step = 0.1
cutoff_sq = 16.0
force_scale = 4.0
length_floor = 0.25


def passed_along(array, axis, by):
    length = lax.axis_size(axis)
    return lax.ppermute(array, axis, [(i, (i + by) % length) for i in range(length)])


def group_force(own_blocks, halo_data, block_ids, atom_ids, live_flags):
    near_data = jnp.take(own_blocks, block_ids, axis=1)
    far_data = jnp.take(halo_data, atom_ids, axis=1)
    offset_vec = near_data[:3, :, :, None] - far_data[:3, :, None, :]
    dist_sq = jnp.sum(offset_vec * offset_vec, axis=0)
    inverse = 1.0 / (dist_sq + 1.0)
    switch = jnp.maximum(1.0 - dist_sq / cutoff_sq, 0.0) ** 2
    strength = (
        force_scale
        * (2.0 * inverse**3 - near_data[3][:, :, None] * far_data[3][:, None, :] * inverse**2)
        * switch
    )
    forces = jnp.sum(strength[None] * offset_vec, axis=3)
    return forces * live_flags[None, :, None]


def geometry(atom_first, atom_second, mass_first, mass_second):
    offset_vec = atom_first - atom_second
    length = jnp.sqrt(jnp.sum(offset_vec * offset_vec, axis=0) + length_floor)
    return (offset_vec / length, lax.rsqrt(mass_first + mass_second))


def project_bond(direction, bond_scale, atom_first, atom_second):
    return bond_scale * jnp.sum(direction * (atom_first - atom_second), axis=0)


def from_domains(rim_data, row_width):
    strides = (1, -1, row_width, -row_width)
    return jnp.concatenate([passed_along(rim_data, "dom", -stride) for stride in strides], axis=1)


def order_fields(rim_data, row_width):
    strides = (1, -1, row_width, -row_width)
    return jnp.concatenate([passed_along(rim_data, "dom", -stride) for stride in strides], axis=1)


def shards(
    coords,
    velocity,
    charge,
    inv_mass,
    tile_block,
    tile_atoms,
    active_tile_count,
    bond_atoms,
    cross_atoms,
    cross_side,
    cross_count,
):
    atom_count = coords.shape[-1]
    shell_size = atom_count // 2
    row_width = max(2, lax.axis_size("dom") // 8)
    strides = (1, -1, row_width, -row_width)
    coords = coords.reshape(3, atom_count)
    velocity = velocity.reshape(3, atom_count)
    inv_mass = inv_mass.reshape(atom_count)
    tile_block = tile_block.reshape(-1)
    tile_atoms = tile_atoms.reshape(-1, TILE)
    live_tiles = active_tile_count.reshape(())
    bond_left = bond_atoms.reshape(2, -1)[0]
    bond_partner_right = bond_atoms.reshape(2, -1)[1]
    cross_left = cross_atoms.reshape(2, -1)[0]
    cross_right = cross_atoms.reshape(2, -1)[1]
    side_code = cross_side.reshape(-1)
    slot_count = side_code.shape[0]
    cross_live = jnp.arange(slot_count, dtype=jnp.int32) < cross_count.reshape(())
    cross_flag = cross_live.astype(jnp.float32)
    own_data = jnp.concatenate([coords, charge.reshape(1, atom_count), inv_mass[None]], axis=0)
    outer_rim = own_data[:, :shell_size]
    slab_pieces = [passed_along(outer_rim, "slab", stride) for stride in (1, -1)]
    halo_data = jnp.concatenate(
        [own_data, from_domains(outer_rim, row_width)] + slab_pieces, axis=1
    )
    tiles = tile_atoms.shape[0]
    group_size = min(16, tiles)
    grouped = tiles // group_size
    block_count = atom_count // TILE
    own_blocks = own_data.reshape(5, block_count, TILE)
    tile_flags = (jnp.arange(tiles, dtype=jnp.int32) < live_tiles).astype(jnp.float32)
    block_range = jnp.arange(block_count, dtype=jnp.int32)

    def add_group(group, totals):
        start = group * group_size
        block_ids = lax.dynamic_slice_in_dim(tile_block, start, group_size, 0)
        atom_ids = lax.dynamic_slice_in_dim(tile_atoms, start, group_size, 0)
        live_flags = lax.dynamic_slice_in_dim(tile_flags, start, group_size, 0)
        group_values = group_force(own_blocks, halo_data, block_ids, atom_ids, live_flags)
        pick_entries = (block_ids[:, None] == block_range[None, :]).astype(jnp.float32)
        return totals + jnp.einsum(
            "gb,agx->abx", pick_entries, group_values, precision=lax.Precision.HIGHEST
        )

    force_blocks = lax.fori_loop(
        0, grouped, add_group, jnp.zeros((3, block_count, TILE), jnp.float32)
    )
    forces = force_blocks.reshape(3, atom_count)
    velocity_half = velocity + time_step * forces * inv_mass[None]
    displace = time_step * velocity_half
    updated_positions = coords + displace
    far_data = halo_data[:, atom_count : atom_count + 4 * shell_size]
    local_dir, local_scale = geometry(
        coords[:, bond_left],
        coords[:, bond_partner_right],
        inv_mass[bond_left],
        inv_mass[bond_partner_right],
    )
    cross_index = side_code * shell_size + cross_right
    cross_dir, cross_scale = geometry(
        coords[:, cross_left],
        far_data[:3, cross_index],
        inv_mass[cross_left],
        far_data[4, cross_index],
    )
    displace_far = from_domains(displace[:, :shell_size], row_width)
    local_rhs = project_bond(
        local_dir, local_scale, displace[:, bond_left], displace[:, bond_partner_right]
    )
    cross_rhs = (
        project_bond(cross_dir, cross_scale, displace[:, cross_left], displace_far[:, cross_index])
        * cross_flag
    )
    residue = (local_rhs, cross_rhs)

    def collect(values):
        pushed = local_dir * (local_scale * values[0])
        totals = (
            jnp.zeros((3, atom_count), jnp.float32)
            .at[:, bond_left]
            .add(pushed)
            .at[:, bond_partner_right]
            .add(-pushed)
        )
        cross_push = cross_dir * (cross_scale * values[1])
        totals = totals.at[:, cross_left].add(cross_push)
        outward = jnp.zeros((3, 4 * shell_size), jnp.float32).at[:, cross_index].add(-cross_push)
        returned = [
            passed_along(
                outward[:, neighbour * shell_size : (neighbour + 1) * shell_size],
                "dom",
                strides[neighbour],
            )
            for neighbour in range(4)
        ]
        arrived = returned[0] + returned[1] + returned[2] + returned[3]
        totals = totals + jnp.pad(arrived, ((0, 0), (0, atom_count - shell_size)))
        return inv_mass[None] * totals

    def changes(spread_now, far_cross):
        local_change = project_bond(
            local_dir, local_scale, spread_now[:, bond_left], spread_now[:, bond_partner_right]
        )
        cross_change = (
            project_bond(cross_dir, cross_scale, spread_now[:, cross_left], far_cross) * cross_flag
        )
        return (local_change, cross_change)

    accumulated_sum = residue
    for expansion in range(ORDER):
        spread_now = collect(residue)
        spread_far = order_fields(spread_now[:, :shell_size], row_width)
        far_cross = spread_far[:, cross_index]
        residue = tuple(
            (
                value_now - value_step
                for value_now, value_step in zip(residue, changes(spread_now, far_cross))
            )
        )
        accumulated_sum = tuple(
            (value_sum + value_now for value_sum, value_now in zip(accumulated_sum, residue))
        )
    correction = collect(accumulated_sum)
    coords_out = (updated_positions - correction).reshape(3, 1, 1, atom_count)
    velocity_out = (velocity_half - correction / time_step).reshape(3, 1, 1, atom_count)
    return (coords_out, velocity_out)


def solution(mesh):
    return jax.shard_map(
        shards,
        mesh=mesh,
        in_specs=(
            P(None, "slab", "dom", None),
            P(None, "slab", "dom", None),
            P("slab", "dom", None),
            P("slab", "dom", None),
            P("slab", "dom", None),
            P("slab", "dom", None, None),
            P("slab", "dom"),
            P(None, "slab", "dom", None),
            P(None, "slab", "dom", None),
            P("slab", "dom", None),
            P("slab", "dom"),
        ),
        out_specs=(P(None, "slab", "dom", None), P(None, "slab", "dom", None)),
        check_vma=False,
    )
```

profile of v0, /device:TPU:14, one launch (start us, length us, event | category | flops | bytes accessed | tf_op | source)
XLA Modules:
  0.0 573.9 jit_solution(6255685030605329914)
XLA Ops:
  2.4 21.0 %collective-permute-start = (f32[5,256]{1,0:T(8,128)S(1)}, f32[5,256]{1,0:T(8,128)S(1)}, u32[]{:S(2)}, u32[]{:S(2)}) collective-permute-start(f32[5,256]{1,0:T(8,128)S(1)} %slice.228), channel_id=1, source_target_pairs={{0,63},{1,0},{2,1},{3,2},{4,3},{5,4},{6,5},{7,6},{8,7},{9,8},{10,9... | collective-permute-start | bytes 15368 | tf_op jit(solution)/shard_map/ppermute | solution.py:18
  45.2 42.0 %while.16 = (s32[]{:T(128)}, f32[3,4,128]{2,1,0:T(4,128)S(1)}, s32[64]{0:T(128)S(1)}, f32[5,4,128]{2,0,1:T(8,128)S(1)}, s32[64,128]{1,0:T(8,128)S(1)}, /*index=5...) while((s32[]{:T(128)}, f32[3,4,128]{2,1,0:T(4,128)S(1)}, ...), condition=%wide.region_3.4_spmd.clone, body=%wide.region_0.3_spmd.clone.sunk | while | flops 8466647 | bytes 5002069 | solution.py:113
  46.1 5.5 gather_fusion
  56.5 5.5 gather_fusion
  67.0 5.5 gather_fusion
  77.5 5.5 gather_fusion
  89.0 8.5 %collective-permute-start.6 = (f32[3,256]{0,1:T(8,128)S(1)}, f32[3,256]{0,1:T(8,128)S(1)}, u32[]{:S(2)}, u32[]{:S(2)}) collective-permute-start(f32[3,256]{0,1:T(8,128)S(1)} %slice.229), channel_id=1, source_target_pairs={{0,63},{1,0},{2,1},{3,2},{4,3},{5,4},{6,5},{7,6},{8,7},{9,8},{10,9... | collective-permute-start | bytes 9224 | tf_op jit(solution)/shard_map/ppermute | solution.py:18
  105.5 244.1 %while.15 = (s32[]{:T(128)}, f32[5,1024]{0,1:T(8,128)S(1)}, s32[128,2]{0,1:T(2,128)S(1)}, f32[128,3]{1,0:T(8,128)S(1)}, s32[]{:T(128)}, /*index=5*/s32[]{:T(128)}) while((s32[]{:T(128)}, f32[5,1024]{0,1:T(8,128)S(1)}, s32[128,2]{0,1:T(2,128)S(1)}, f32[128,3]{1,0:T(8,128)S(1)}, s32[]{:T(128)}, /*index=5*/s32[]{:T(128)}) %tuple.100), condition=%wide.while_cond, body=%wide.while_body.sunk | while | flops 2 | bytes 165 | solution.py:130
  355.9 8.4 %collective-permute-start.11 = (f32[3,256]{0,1:T(8,128)S(1)}, f32[3,256]{0,1:T(8,128)S(1)}, u32[]{:S(2)}, u32[]{:S(2)}) collective-permute-start(f32[3,256]{0,1:T(8,128)S(1)} %get-tuple-element.283), channel_id=1, source_target_pairs={{0,63},{1,0},{2,1},{3,2},{4,3},{5,4},{6,5},{7,6},{8,7},{9,8},{10,9... | collective-permute-start | bytes 9224 | tf_op jit(solution)/shard_map/ppermute | solution.py:18
  366.3 5.1 collective-permute-start.13
  388.2 5.1 collective-permute-start.16
  405.5 7.2 %collective-permute-start.19 = (f32[3,256]{0,1:T(8,128)S(1)}, f32[3,256]{0,1:T(8,128)S(1)}, u32[]{:S(2)}, u32[]{:S(2)}) collective-permute-start(f32[3,256]{0,1:T(8,128)S(1)} %get-tuple-element.279), channel_id=1, source_target_pairs={{0,63},{1,0},{2,1},{3,2},{4,3},{5,4},{6,5},{7,6},{8,7},{9,8},{10,9... | collective-permute-start | bytes 9224 | tf_op jit(solution)/shard_map/ppermute | solution.py:18
  414.7 5.1 collective-permute-start.21
  436.1 5.1 collective-permute-start.24
  453.5 7.2 %collective-permute-start.27 = (f32[3,256]{0,1:T(8,128)S(1)}, f32[3,256]{0,1:T(8,128)S(1)}, u32[]{:S(2)}, u32[]{:S(2)}) collective-permute-start(f32[3,256]{0,1:T(8,128)S(1)} %get-tuple-element.275), channel_id=1, source_target_pairs={{0,63},{1,0},{2,1},{3,2},{4,3},{5,4},{6,5},{7,6},{8,7},{9,8},{10,9... | collective-permute-start | bytes 9224 | tf_op jit(solution)/shard_map/ppermute | solution.py:18
  462.6 5.1 collective-permute-start.29
  484.1 5.1 collective-permute-start.32
  492.3 5.0 collective-permute-done.33
  501.4 7.2 %collective-permute-start.35 = (f32[3,256]{0,1:T(8,128)S(1)}, f32[3,256]{0,1:T(8,128)S(1)}, u32[]{:S(2)}, u32[]{:S(2)}) collective-permute-start(f32[3,256]{0,1:T(8,128)S(1)} %get-tuple-element.271), channel_id=1, source_target_pairs={{0,63},{1,0},{2,1},{3,2},{4,3},{5,4},{6,5},{7,6},{8,7},{9,8},{10,9... | collective-permute-start | bytes 9224 | tf_op jit(solution)/shard_map/ppermute | solution.py:18
  510.8 5.1 collective-permute-start.37
  532.3 5.1 collective-permute-start.40
  540.5 5.0 collective-permute-done.41
  550.9 5.9 %collective-permute-start.43 = (f32[3,256]{0,1:T(8,128)S(1)}, f32[3,256]{0,1:T(8,128)S(1)}, u32[]{:S(2)}, u32[]{:S(2)}) collective-permute-start(f32[3,256]{0,1:T(8,128)S(1)} %get-tuple-element.267), channel_id=1, source_target_pairs={{0,63},{1,0},{2,1},{3,2},{4,3},{5,4},{6,5},{7,6},{8,7},{9,8},{10,9... | collective-permute-start | bytes 9224 | tf_op jit(solution)/shard_map/ppermute | solution.py:18
  558.8 5.1 collective-permute-start.45
  (808 shorter events, 426.1 us)
Async XLA Ops:
  2.4 39.3 %collective-permute-start = (f32[5,256]{1,0:T(8,128)S(1)}, f32[5,256]{1,0:T(8,128)S(1)}, u32[]{:S(2)}, u32[]{:S(2)}) collective-permute-start(f32[5,256]{1,0:T(8,128)S(1)} %slice.228), channel_id=1, source_target_pairs={{0,63},{1,0},{2,1},{3,2},{4,3},{5,4},{6,5},{7,6},{8,7},{9,8},{10,9... | collective-permute-start | bytes 15368 | tf_op jit(solution)/shard_map/ppermute | solution.py:18
  23.4 20.1 %collective-permute-start.1 = (f32[5,256]{1,0:T(8,128)S(1)}, f32[5,256]{1,0:T(8,128)S(1)}, u32[]{:S(2)}, u32[]{:S(2)}) collective-permute-start(f32[5,256]{1,0:T(8,128)S(1)} %slice.228), channel_id=1, source_target_pairs={{0,1},{1,2},{2,3},{3,4},{4,5},{5,6},{6,7},{7,8},{8,9},{9,10},{10,1... | collective-permute-start | bytes 15368 | tf_op jit(solution)/shard_map/ppermute | solution.py:18
  25.3 18.1 %collective-permute-start.2 = (f32[5,256]{1,0:T(8,128)S(1)}, f32[5,256]{1,0:T(8,128)S(1)}, u32[]{:S(2)}, u32[]{:S(2)}) collective-permute-start(f32[5,256]{1,0:T(8,128)S(1)} %slice.228), channel_id=1, source_target_pairs={{0,56},{1,57},{2,58},{3,59},{4,60},{5,61},{6,62},{7,63},{8,0},{9,1... | collective-permute-start | bytes 15368 | tf_op jit(solution)/shard_map/ppermute | solution.py:18
  28.5 15.0 %collective-permute-start.3 = (f32[5,256]{1,0:T(8,128)S(1)}, f32[5,256]{1,0:T(8,128)S(1)}, u32[]{:S(2)}, u32[]{:S(2)}) collective-permute-start(f32[5,256]{1,0:T(8,128)S(1)} %slice.228), channel_id=1, source_target_pairs={{0,8},{1,9},{2,10},{3,11},{4,12},{5,13},{6,14},{7,15},{8,16},{9,17... | collective-permute-start | bytes 15368 | tf_op jit(solution)/shard_map/ppermute | solution.py:18
  31.2 12.3 %collective-permute-start.4 = (f32[5,256]{1,0:T(8,128)S(1)}, f32[5,256]{1,0:T(8,128)S(1)}, u32[]{:S(2)}, u32[]{:S(2)}) collective-permute-start(f32[5,256]{1,0:T(8,128)S(1)} %slice.228), channel_id=1, source_target_pairs={{0,64},{64,128},{128,192},{192,256},{256,320},{320,384},{384,448},... | collective-permute-start | bytes 15368 | tf_op jit(solution)/shard_map/ppermute | solution.py:18
  89.0 262.8 %collective-permute-start.6 = (f32[3,256]{0,1:T(8,128)S(1)}, f32[3,256]{0,1:T(8,128)S(1)}, u32[]{:S(2)}, u32[]{:S(2)}) collective-permute-start(f32[3,256]{0,1:T(8,128)S(1)} %slice.229), channel_id=1, source_target_pairs={{0,63},{1,0},{2,1},{3,2},{4,3},{5,4},{6,5},{7,6},{8,7},{9,8},{10,9... | collective-permute-start | bytes 9224 | tf_op jit(solution)/shard_map/ppermute | solution.py:18
  97.4 254.3 %collective-permute-start.7 = (f32[3,256]{0,1:T(8,128)S(1)}, f32[3,256]{0,1:T(8,128)S(1)}, u32[]{:S(2)}, u32[]{:S(2)}) collective-permute-start(f32[3,256]{0,1:T(8,128)S(1)} %slice.229), channel_id=1, source_target_pairs={{0,1},{1,2},{2,3},{3,4},{4,5},{5,6},{6,7},{7,8},{8,9},{9,10},{10,1... | collective-permute-start | bytes 9224 | tf_op jit(solution)/shard_map/ppermute | solution.py:18
  99.4 252.4 %collective-permute-start.8 = (f32[3,256]{0,1:T(8,128)S(1)}, f32[3,256]{0,1:T(8,128)S(1)}, u32[]{:S(2)}, u32[]{:S(2)}) collective-permute-start(f32[3,256]{0,1:T(8,128)S(1)} %slice.229), channel_id=1, source_target_pairs={{0,56},{1,57},{2,58},{3,59},{4,60},{5,61},{6,62},{7,63},{8,0},{9,1... | collective-permute-start | bytes 9224 | tf_op jit(solution)/shard_map/ppermute | solution.py:18
  101.3 250.5 %collective-permute-start.9 = (f32[3,256]{0,1:T(8,128)S(1)}, f32[3,256]{0,1:T(8,128)S(1)}, u32[]{:S(2)}, u32[]{:S(2)}) collective-permute-start(f32[3,256]{0,1:T(8,128)S(1)} %slice.229), channel_id=1, source_target_pairs={{0,8},{1,9},{2,10},{3,11},{4,12},{5,13},{6,14},{7,15},{8,16},{9,17... | collective-permute-start | bytes 9224 | tf_op jit(solution)/shard_map/ppermute | solution.py:18
  354.0 17.5 %collective-permute-start.10 = (f32[3,256]{0,1:T(8,128)S(1)}, f32[3,256]{0,1:T(8,128)S(1)}, u32[]{:S(2)}, u32[]{:S(2)}) collective-permute-start(f32[3,256]{0,1:T(8,128)S(1)} %get-tuple-element.286), channel_id=1, source_target_pairs={{0,1},{1,2},{2,3},{3,4},{4,5},{5,6},{6,7},{7,8},{8,9},{9,10},{10,1... | collective-permute-start | bytes 9224 | tf_op jit(solution)/shard_map/ppermute | solution.py:18
  355.9 15.6 %collective-permute-start.11 = (f32[3,256]{0,1:T(8,128)S(1)}, f32[3,256]{0,1:T(8,128)S(1)}, u32[]{:S(2)}, u32[]{:S(2)}) collective-permute-start(f32[3,256]{0,1:T(8,128)S(1)} %get-tuple-element.283), channel_id=1, source_target_pairs={{0,63},{1,0},{2,1},{3,2},{4,3},{5,4},{6,5},{7,6},{8,7},{9,8},{10,9... | collective-permute-start | bytes 9224 | tf_op jit(solution)/shard_map/ppermute | solution.py:18
  381.9 14.4 %collective-permute-start.14 = (f32[3,256]{0,1:T(8,128)S(1)}, f32[3,256]{0,1:T(8,128)S(1)}, u32[]{:S(2)}, u32[]{:S(2)}) collective-permute-start(f32[3,256]{0,1:T(8,128)S(1)} %slice.234), channel_id=1, source_target_pairs={{0,63},{1,0},{2,1},{3,2},{4,3},{5,4},{6,5},{7,6},{8,7},{9,8},{10,9... | collective-permute-start | bytes 9224 | tf_op jit(solution)/shard_map/ppermute | solution.py:18
  403.6 16.3 %collective-permute-start.18 = (f32[3,256]{0,1:T(8,128)S(1)}, f32[3,256]{0,1:T(8,128)S(1)}, u32[]{:S(2)}, u32[]{:S(2)}) collective-permute-start(f32[3,256]{0,1:T(8,128)S(1)} %get-tuple-element.282), channel_id=1, source_target_pairs={{0,1},{1,2},{2,3},{3,4},{4,5},{5,6},{6,7},{7,8},{8,9},{9,10},{10,1... | collective-permute-start | bytes 9224 | tf_op jit(solution)/shard_map/ppermute | solution.py:18
  405.5 14.3 %collective-permute-start.19 = (f32[3,256]{0,1:T(8,128)S(1)}, f32[3,256]{0,1:T(8,128)S(1)}, u32[]{:S(2)}, u32[]{:S(2)}) collective-permute-start(f32[3,256]{0,1:T(8,128)S(1)} %get-tuple-element.279), channel_id=1, source_target_pairs={{0,63},{1,0},{2,1},{3,2},{4,3},{5,4},{6,5},{7,6},{8,7},{9,8},{10,9... | collective-permute-start | bytes 9224 | tf_op jit(solution)/shard_map/ppermute | solution.py:18
  429.9 14.2 %collective-permute-start.22 = (f32[3,256]{0,1:T(8,128)S(1)}, f32[3,256]{0,1:T(8,128)S(1)}, u32[]{:S(2)}, u32[]{:S(2)}) collective-permute-start(f32[3,256]{0,1:T(8,128)S(1)} %slice.239), channel_id=1, source_target_pairs={{0,63},{1,0},{2,1},{3,2},{4,3},{5,4},{6,5},{7,6},{8,7},{9,8},{10,9... | collective-permute-start | bytes 9224 | tf_op jit(solution)/shard_map/ppermute | solution.py:18
  434.2 10.9 %collective-permute-start.23 = (f32[3,256]{0,1:T(8,128)S(1)}, f32[3,256]{0,1:T(8,128)S(1)}, u32[]{:S(2)}, u32[]{:S(2)}) collective-permute-start(f32[3,256]{0,1:T(8,128)S(1)} %slice.239), channel_id=1, source_target_pairs={{0,1},{1,2},{2,3},{3,4},{4,5},{5,6},{6,7},{7,8},{8,9},{9,10},{10,1... | collective-permute-start | bytes 9224 | tf_op jit(solution)/shard_map/ppermute | solution.py:18
  451.5 16.3 %collective-permute-start.26 = (f32[3,256]{0,1:T(8,128)S(1)}, f32[3,256]{0,1:T(8,128)S(1)}, u32[]{:S(2)}, u32[]{:S(2)}) collective-permute-start(f32[3,256]{0,1:T(8,128)S(1)} %get-tuple-element.278), channel_id=1, source_target_pairs={{0,1},{1,2},{2,3},{3,4},{4,5},{5,6},{6,7},{7,8},{8,9},{9,10},{10,1... | collective-permute-start | bytes 9224 | tf_op jit(solution)/shard_map/ppermute | solution.py:18
  453.5 14.3 %collective-permute-start.27 = (f32[3,256]{0,1:T(8,128)S(1)}, f32[3,256]{0,1:T(8,128)S(1)}, u32[]{:S(2)}, u32[]{:S(2)}) collective-permute-start(f32[3,256]{0,1:T(8,128)S(1)} %get-tuple-element.275), channel_id=1, source_target_pairs={{0,63},{1,0},{2,1},{3,2},{4,3},{5,4},{6,5},{7,6},{8,7},{9,8},{10,9... | collective-permute-start | bytes 9224 | tf_op jit(solution)/shard_map/ppermute | solution.py:18
  477.8 14.2 %collective-permute-start.30 = (f32[3,256]{0,1:T(8,128)S(1)}, f32[3,256]{0,1:T(8,128)S(1)}, u32[]{:S(2)}, u32[]{:S(2)}) collective-permute-start(f32[3,256]{0,1:T(8,128)S(1)} %slice.244), channel_id=1, source_target_pairs={{0,63},{1,0},{2,1},{3,2},{4,3},{5,4},{6,5},{7,6},{8,7},{9,8},{10,9... | collective-permute-start | bytes 9224 | tf_op jit(solution)/shard_map/ppermute | solution.py:18
  499.5 16.5 %collective-permute-start.34 = (f32[3,256]{0,1:T(8,128)S(1)}, f32[3,256]{0,1:T(8,128)S(1)}, u32[]{:S(2)}, u32[]{:S(2)}) collective-permute-start(f32[3,256]{0,1:T(8,128)S(1)} %get-tuple-element.274), channel_id=1, source_target_pairs={{0,1},{1,2},{2,3},{3,4},{4,5},{5,6},{6,7},{7,8},{8,9},{9,10},{10,1... | collective-permute-start | bytes 9224 | tf_op jit(solution)/shard_map/ppermute | solution.py:18
  501.4 14.6 %collective-permute-start.35 = (f32[3,256]{0,1:T(8,128)S(1)}, f32[3,256]{0,1:T(8,128)S(1)}, u32[]{:S(2)}, u32[]{:S(2)}) collective-permute-start(f32[3,256]{0,1:T(8,128)S(1)} %get-tuple-element.271), channel_id=1, source_target_pairs={{0,63},{1,0},{2,1},{3,2},{4,3},{5,4},{6,5},{7,6},{8,7},{9,8},{10,9... | collective-permute-start | bytes 9224 | tf_op jit(solution)/shard_map/ppermute | solution.py:18
  526.0 14.2 %collective-permute-start.38 = (f32[3,256]{0,1:T(8,128)S(1)}, f32[3,256]{0,1:T(8,128)S(1)}, u32[]{:S(2)}, u32[]{:S(2)}) collective-permute-start(f32[3,256]{0,1:T(8,128)S(1)} %slice.249), channel_id=1, source_target_pairs={{0,63},{1,0},{2,1},{3,2},{4,3},{5,4},{6,5},{7,6},{8,7},{9,8},{10,9... | collective-permute-start | bytes 9224 | tf_op jit(solution)/shard_map/ppermute | solution.py:18
  547.7 16.3 %collective-permute-start.42 = (f32[3,256]{0,1:T(8,128)S(1)}, f32[3,256]{0,1:T(8,128)S(1)}, u32[]{:S(2)}, u32[]{:S(2)}) collective-permute-start(f32[3,256]{0,1:T(8,128)S(1)} %get-tuple-element.270), channel_id=1, source_target_pairs={{0,1},{1,2},{2,3},{3,4},{4,5},{5,6},{6,7},{7,8},{8,9},{9,10},{10,1... | collective-permute-start | bytes 9224 | tf_op jit(solution)/shard_map/ppermute | solution.py:18
  550.9 13.0 %collective-permute-start.43 = (f32[3,256]{0,1:T(8,128)S(1)}, f32[3,256]{0,1:T(8,128)S(1)}, u32[]{:S(2)}, u32[]{:S(2)}) collective-permute-start(f32[3,256]{0,1:T(8,128)S(1)} %get-tuple-element.267), channel_id=1, source_target_pairs={{0,63},{1,0},{2,1},{3,2},{4,3},{5,4},{6,5},{7,6},{8,7},{9,8},{10,9... | collective-permute-start | bytes 9224 | tf_op jit(solution)/shard_map/ppermute | solution.py:18
  (30 other events, 367.3 us)
where the time goes:
time: 582 us; the launch traced here: 574 us
  local copies, waits for them, and re-layouts  295 us (51%)
  starting transfers between devices  183 us (31%)
  other arithmetic  55.6 us (10%)
  waiting for transfers between devices  35 us (6%)
    gather x512, local copies, waits for them, and re-layouts  243 us
    ppermute x46, starting transfers between devices, passed_along(): lax.ppermute(array, axis, [(i, (i + by) % length) for i in range(length)])  183 us
    ppermute x46, waiting for transfers between devices, passed_along(): lax.ppermute(array, axis, [(i, (i + by) % length) for i in range(length)])  35 us
    gather x8, local copies, waits for them, and re-layouts, group_force(): far_data = jnp.take(halo_data, atom_ids, axis=1)  23.2 us
    scatter-add x10, other arithmetic, collect(): totals = jnp.zeros((3, atom_count), jnp.float32).at[:, bond_left].add(pus...  21.8 us
  transfers between devices with their start and end apart: 46, of which 19 were waited for; matrix products, arithmetic and copies ran while one was open for 45% of the time, Pallas kernels for 0%

commit v1 on v0

v1 whole, which is shorter than its diff:
```python
import functools

import jax
import jax.numpy as jnp
from jax import lax
from jax.experimental import pallas as pl
from jax.experimental.pallas import tpu as pltpu
from jax.sharding import PartitionSpec as P

TILE = 128
ORDER = 4
GROUP = 8

time_step = 0.1
cutoff_sq = 16.0
force_scale = 4.0
length_floor = 0.25

MESH = pl.DeviceIdType.MESH
f32, bf16, i32 = jnp.float32, jnp.bfloat16, jnp.int32

MASS, NORM, ONE, CHARGE = 3, 4, 5, 6


def parts3(a):
    high = a.astype(bf16).astype(f32)
    rest = a - high
    mid = rest.astype(bf16).astype(f32)
    low = (rest - mid).astype(bf16).astype(f32)
    return high, mid, low


def lanes(table, index):
    return jnp.take_along_axis(table, index, axis=1, mode="promise_in_bounds")


def row_ids():
    return lax.broadcasted_iota(i32, (8, TILE), 0)


def packed(low, high):
    return jnp.where(row_ids() < 4, low, pltpu.roll(high, 4, 0))


def half(picked, group):
    return jnp.where((group & 1) == 1, pltpu.roll(picked, 4, 0), picked)


def from_packed(tables, index):
    low, group = index & (TILE - 1), index >> 7
    picked = lanes(tables[0], low)
    for k in range(1, len(tables)):
        picked = jnp.where((group >> 1) == k, lanes(tables[k], low), picked)
    return half(picked, group)


def spread_row(row):
    return jnp.broadcast_to(row, (8, TILE))


def direction(first, second, mask):
    offset = jnp.where(row_ids() < 3, first - second, 0.0)
    squared = jnp.sum(offset * offset, axis=0, keepdims=True)
    masses = (first + second)[MASS : MASS + 1, :]
    return offset * (lax.rsqrt(squared + length_floor) * lax.rsqrt(masses) * mask)


def project(scaled_dir, first, second):
    return jnp.sum(scaled_dir * (first - second), axis=0, keepdims=True)


def kernel(
    n_slab,
    n_dom,
    coords_ref,
    velocity_ref,
    charge_ref,
    mass_ref,
    block_ref,
    atoms_ref,
    live_ref,
    bond_ref,
    cross_ref,
    side_ref,
    cross_count_ref,
    coords_out_ref,
    velocity_out_ref,
    own_ref,
    speed_ref,
    halo_ref,
    slots_ref,
    their_slots_ref,
    near_ref,
    far_ref,
    far2_ref,
    bond_inc_ref,
    cross_inc_ref,
    field_ref,
    fields_in_ref,
    halo_send,
    halo_recv,
    slots_send,
    slots_recv,
    field_send,
    field_recv,
):
    slab, dom = lax.axis_index("slab"), lax.axis_index("dom")
    width = max(2, n_dom // 8)
    strides = (1, -1, width, -width)
    in_slab = [(slab, lax.rem(dom + n_dom - s, n_dom)) for s in strides]
    across = [(lax.rem(slab + n_slab + s, n_slab), dom) for s in (1, -1)]
    targets = in_slab + across

    barrier = pltpu.get_barrier_semaphore()
    for target in targets:
        pl.semaphore_signal(barrier, inc=1, device_id=target, device_id_type=MESH)

    x, y, z = (coords_ref[c, 0] for c in range(3))
    own_ref[0:1, :] = x
    own_ref[1:2, :] = y
    own_ref[2:3, :] = z
    own_ref[MASS : MASS + 1, :] = mass_ref[0]
    own_ref[NORM : NORM + 1, :] = x * x + y * y + z * z
    own_ref[ONE : ONE + 1, :] = jnp.ones_like(x)
    own_ref[CHARGE : CHARGE + 1, :] = charge_ref[0]
    own_ref[7:8, :] = jnp.zeros_like(x)
    slots_ref[...] = jnp.zeros_like(slots_ref)
    slots_ref[0:1, :] = cross_ref[0, 0]
    slots_ref[1:2, :] = cross_ref[1, 0]
    slot_ids = lax.broadcasted_iota(i32, (1, TILE), 1)
    slots_ref[2:3, :] = jnp.where(slot_ids < cross_count_ref[0, 0], side_ref[0], 8)

    pl.semaphore_wait(barrier, len(targets))
    copies = []
    halo_copies, slot_copies = [], []
    for n, target in enumerate(targets):
        halo_copies.append(
            pltpu.make_async_remote_copy(
                src_ref=own_ref.at[:, pl.ds(0, 2 * TILE)],
                dst_ref=halo_ref.at[n],
                send_sem=halo_send.at[n],
                recv_sem=halo_recv.at[n],
                device_id=target,
                device_id_type=MESH,
            )
        )
        halo_copies[-1].start()
    for n, target in enumerate(in_slab):
        slot_copies.append(
            pltpu.make_async_remote_copy(
                src_ref=slots_ref,
                dst_ref=their_slots_ref.at[n],
                send_sem=slots_send.at[n],
                recv_sem=slots_recv.at[n],
                device_id=target,
                device_id_type=MESH,
            )
        )
        slot_copies[-1].start()
    copies += halo_copies + slot_copies

    own = own_ref[...]
    rows = lax.broadcasted_iota(i32, own.shape, 0)
    norm = own[NORM : NORM + 1, :]
    distance = jnp.where(rows < 3, -2.0 * own, 0.0)
    distance = jnp.where(rows == NORM, 1.0, distance)
    distance = jnp.where(rows == ONE, norm + 1.0, distance)
    charges = jnp.where(rows == CHARGE, force_scale * own, 0.0)
    for half_at, table in enumerate((distance, charges)):
        h, m, l = parts3(table)
        near = jnp.transpose(jnp.concatenate([h, m, l, h, m, h], axis=0)).astype(bf16)
        for b in range(4):
            near_ref[b, half_at * TILE : (half_at + 1) * TILE, :] = near[
                b * TILE : (b + 1) * TILE, :
            ]

    own_packed = [packed(own[:, 2 * k * TILE : (2 * k + 1) * TILE], own[:, (2 * k + 1) * TILE : (2 * k + 2) * TILE]) for k in range(2)]
    ones = jnp.ones((1, TILE), f32)
    bond_ends, bond_dir = [], []
    atom_ids = lax.broadcasted_iota(i32, (TILE, 4 * TILE), 1).astype(f32)
    for g in range(2):
        ends = [spread_row(bond_ref[e, 0][:, g * TILE : (g + 1) * TILE]) for e in range(2)]
        bond_ends.append(ends)
        bond_dir.append(direction(*[from_packed(own_packed, e) for e in ends], ones))
        columns = [jnp.transpose(e.astype(f32))[:, 0:1] for e in ends]
        marks = [jnp.where(c == atom_ids, 1.0, 0.0) for c in columns]
        bond_inc_ref[g * TILE : (g + 1) * TILE, :] = (marks[0] - marks[1]).astype(bf16)

    for copy in slot_copies:
        copy.wait_recv()
    tables = [slots_ref[...]] + [their_slots_ref[n] for n in range(4)]
    cross_own, cross_far, masks = [], [], []
    sides = spread_row(tables[0][2:3, :])
    for n, table in enumerate(tables):
        mine, theirs = (0, 1) if n == 0 else (1, 0)
        cross_own.append(spread_row(table[mine : mine + 1, :]))
        cross_far.append(spread_row(table[theirs : theirs + 1, :]))
        code = table[2:3, :]
        alive = code < 4 if n == 0 else code == ((n - 1) ^ 1)
        masks.append(jnp.where(alive, 1.0, 0.0))
        column = jnp.transpose(cross_own[-1].astype(f32))[:, 0:1]
        cross_inc_ref[n * TILE : (n + 1) * TILE, :] = jnp.where(
            column == atom_ids[:, : 2 * TILE], 1.0, 0.0
        ).astype(bf16)

    for copy in halo_copies:
        copy.wait_recv()

    def far_ends(tables):
        low, group = cross_far[0] & (TILE - 1), cross_far[0] >> 7
        picked = lanes(tables[0], low)
        for k in range(1, 4):
            picked = jnp.where(sides == k, lanes(tables[k], low), picked)
        return [half(picked, group)] + [from_packed([tables[n]], cross_far[n + 1]) for n in range(4)]

    far_packed = [packed(halo_ref[n, :, 0:TILE], halo_ref[n, :, TILE : 2 * TILE]) for n in range(4)]
    near_ends = [from_packed(own_packed[:1], c) for c in cross_own]
    cross_dir = [direction(a, b, m) for a, b, m in zip(near_ends, far_ends(far_packed), masks)]

    def gather(group, carry):
        index = atoms_ref[0, 0, pl.ds(pl.multiple_of(group * GROUP, GROUP), GROUP), :]
        tables = [own_ref[:, g * TILE : (g + 1) * TILE] for g in range(4)]
        tables += [halo_ref[n, :, g * TILE : (g + 1) * TILE] for n in range(6) for g in range(2)]
        for r in range(GROUP):
            entry = spread_row(index[r : r + 1, :])
            low = entry & (TILE - 1)
            found = [lanes(t, low) for t in tables]
            for bit in range(4):
                upper = ((entry >> (7 + bit)) & 1) == 1
                found = [jnp.where(upper, b, a) for a, b in zip(found[::2], found[1::2])]
            h, m, l = parts3(found[0])
            far_ref[group * GROUP + r] = jnp.concatenate([h, h, h, m, m, l], axis=0).astype(bf16)
            far2_ref[group * GROUP + r] = jnp.concatenate([h, m], axis=0).astype(bf16)
        return carry

    n_tiles = atoms_ref.shape[2]
    lax.fori_loop(0, n_tiles // GROUP, gather, 0)

    def pairs(group, totals):
        for r in range(GROUP):
            tile = group * GROUP + r
            block = block_ref[0, 0, tile]
            both = jnp.dot(near_ref[block], far_ref[tile], preferred_element_type=f32)
            dist, charge = both[:TILE], both[TILE:]
            inverse = 1.0 / dist
            switch = jnp.maximum((1.0 + 1.0 / cutoff_sq) - dist * (1.0 / cutoff_sq), 0.0)
            strength = (2.0 * force_scale * inverse - charge) * ((inverse * switch) * (inverse * switch))
            high = strength.astype(bf16)
            rest = (strength - high.astype(f32)).astype(bf16)
            summed = lax.dot_general(
                far2_ref[tile],
                jnp.concatenate([high, rest], axis=0),
                (((1,), (1,)), ((), ())),
                preferred_element_type=f32,
            )
            summed = summed[:, :TILE] + summed[:, TILE:]
            summed = summed[:8] + summed[8:]
            alive = jnp.where(tile < live_ref[0, 0], 1, 0)
            totals = tuple(
                t + summed * jnp.where(block == b, alive, 0).astype(f32)
                for b, t in enumerate(totals)
            )
        return totals

    totals = lax.fori_loop(
        0, n_tiles // GROUP, pairs, tuple(jnp.zeros((8, TILE), f32) for _ in range(4))
    )
    totals = jnp.concatenate(totals, axis=1)
    speed_ref[...] = jnp.zeros_like(speed_ref)
    for c in range(3):
        speed_ref[c : c + 1, :] = velocity_ref[c, 0]
    mass = own[MASS : MASS + 1, :]
    force = jnp.where(rows < 3, own * totals[ONE : ONE + 1, :] - totals, 0.0)
    velocity_half = speed_ref[...] + time_step * force * mass
    displace = time_step * velocity_half

    def exchange(step, shell):
        field_ref[step] = shell
        sent = []
        for n, target in enumerate(in_slab):
            sent.append(
                pltpu.make_async_remote_copy(
                    src_ref=field_ref.at[step],
                    dst_ref=fields_in_ref.at[step, n],
                    send_sem=field_send.at[step, n],
                    recv_sem=field_recv.at[step, n],
                    device_id=target,
                    device_id_type=MESH,
                )
            )
            sent[-1].start()
        return sent

    def changes(step, field):
        parts = [field[:, g * TILE : (g + 1) * TILE] for g in range(4)]
        tables = [packed(parts[0], parts[1]), packed(parts[2], parts[3])]
        sent = exchange(step, tables[0])
        copies.extend(sent)
        local = [project(d, from_packed(tables, a), from_packed(tables, b)) for d, (a, b) in zip(bond_dir, bond_ends)]
        here = [from_packed(tables[:1], c) for c in cross_own]
        for copy in sent:
            copy.wait_recv()
        there = far_ends([fields_in_ref[step, n] for n in range(4)])
        return local + [project(d, a, b) for d, a, b in zip(cross_dir, here, there)]

    scaled_dirs = bond_dir + cross_dir

    def spread(values):
        pushed = jnp.concatenate([d * v for d, v in zip(scaled_dirs, values)], axis=1)
        high = pushed.astype(bf16).astype(f32)
        pushed = jnp.concatenate([high, pushed - high], axis=0).astype(bf16)
        bonds = jnp.dot(pushed[:, : 2 * TILE], bond_inc_ref[...], preferred_element_type=f32)
        cross = jnp.dot(pushed[:, 2 * TILE :], cross_inc_ref[...], preferred_element_type=f32)
        total = jnp.concatenate([bonds[:, : 2 * TILE] + cross, bonds[:, 2 * TILE :]], axis=1)
        return (total[:8] + total[8:]) * mass

    residue = changes(0, displace)
    summed = residue
    for step in range(1, ORDER + 1):
        residue = [r - c for r, c in zip(residue, changes(step, spread(residue)))]
        summed = [s + r for s, r in zip(summed, residue)]
    correction = spread(summed)
    coords_out = own + displace - correction
    velocity_out = velocity_half - correction * (1.0 / time_step)
    for c in range(3):
        coords_out_ref[c, 0] = coords_out[c : c + 1, :]
        velocity_out_ref[c, 0] = velocity_out[c : c + 1, :]
    for copy in copies:
        copy.wait_send()


def shards(coords, velocity, charge, inv_mass, tile_block, tile_atoms, active_tile_count, bond_atoms, cross_atoms, cross_side, cross_count):
    n_slab, n_dom = lax.axis_size("slab"), lax.axis_size("dom")
    atoms = coords.shape[-1]
    tiles = tile_atoms.shape[2]
    vmem, smem = pl.BlockSpec(memory_space=pltpu.VMEM), pl.BlockSpec(memory_space=pltpu.SMEM)
    shape = jax.ShapeDtypeStruct(coords.shape, f32)
    return pl.pallas_call(
        functools.partial(kernel, n_slab, n_dom),
        out_shape=(shape, shape),
        in_specs=[vmem, vmem, vmem, vmem, smem, vmem, smem, vmem, vmem, vmem, smem],
        out_specs=(vmem, vmem),
        scratch_shapes=[
            pltpu.VMEM((8, atoms), f32),
            pltpu.VMEM((8, atoms), f32),
            pltpu.VMEM((6, 8, 2 * TILE), f32),
            pltpu.VMEM((8, TILE), i32),
            pltpu.VMEM((4, 8, TILE), i32),
            pltpu.VMEM((4, 2 * TILE, 48), bf16),
            pltpu.VMEM((tiles, 48, TILE), bf16),
            pltpu.VMEM((tiles, 16, TILE), bf16),
            pltpu.VMEM((2 * TILE, atoms), bf16),
            pltpu.VMEM((5 * TILE, 2 * TILE), bf16),
            pltpu.VMEM((ORDER + 1, 8, TILE), f32),
            pltpu.VMEM((ORDER + 1, 4, 8, TILE), f32),
            pltpu.SemaphoreType.DMA((6,)),
            pltpu.SemaphoreType.DMA((6,)),
            pltpu.SemaphoreType.DMA((4,)),
            pltpu.SemaphoreType.DMA((4,)),
            pltpu.SemaphoreType.DMA((ORDER + 1, 4)),
            pltpu.SemaphoreType.DMA((ORDER + 1, 4)),
        ],
        compiler_params=pltpu.CompilerParams(collective_id=0, has_side_effects=True),
    )(coords, velocity, charge, inv_mass, tile_block, tile_atoms, active_tile_count, bond_atoms, cross_atoms, cross_side, cross_count)


def solution(mesh):
    return jax.shard_map(
        shards,
        mesh=mesh,
        in_specs=(
            P(None, "slab", "dom", None),
            P(None, "slab", "dom", None),
            P("slab", "dom", None),
            P("slab", "dom", None),
            P("slab", "dom", None),
            P("slab", "dom", None, None),
            P("slab", "dom"),
            P(None, "slab", "dom", None),
            P(None, "slab", "dom", None),
            P("slab", "dom", None),
            P("slab", "dom"),
        ),
        out_specs=(P(None, "slab", "dom", None), P(None, "slab", "dom", None)),
        check_vma=False,
    )
```

time: 582 us -> 59.7 us (0.10); the launches traced: 574 us -> 59.5 us
  local copies, waits for them, and re-layouts: 295 us -> 1.89 us
  starting transfers between devices: 183 us -> 0 us
  Pallas kernels: 0 us -> 55.6 us
  other arithmetic: 55.6 us -> 0 us
  waiting for transfers between devices: 35 us -> 0 us
    gather x551 -> x0, local copies, waits for them, and re-layouts: 291 us -> none
    ppermute x46 -> x0, starting transfers between devices: 183 us -> none  [passed_along(): lax.ppermute(array, axis, [(i, (i + by) % length) for i in range(length)])]
    pallas_call x0 -> x1, Pallas kernels: none -> 55.6 us  [shards(): pl.pallas_call(functools.partial(kernel, n_slab, n_dom), out_shape=(shape...]
    scatter-add x20 -> x0, other arithmetic: 35.3 us -> none  [the longest x10 21.8 us: collect(): totals = jnp.zeros((3, atom_count), jnp.float32).at[:, bond_left].add(pus...]
    ppermute x46 -> x0, waiting for transfers between devices: 35 us -> none  [passed_along(): lax.ppermute(array, axis, [(i, (i + by) % length) for i in range(length)])]
    reduce_sum x20 -> x0, other arithmetic: 13.9 us -> none  [the longest x4 7.7 us: group_force(): forces = jnp.sum(strength[None] * offset_vec, axis=3)]
  transfers between devices with their start and end apart: 46 -> 0, of which waited for: 19 -> 0; matrix products, arithmetic and copies ran while one was open for 45% -> 0% of each run, Pallas kernels for 0% -> 0%
where the time goes in v1:
time: 59.7 us; the launch traced here: 59.5 us
  Pallas kernels  55.6 us (93%)
  between operations  1.94 us (3%)
  local copies, waits for them, and re-layouts  1.89 us (3%)
    pallas_call x1, Pallas kernels, shards(): pl.pallas_call(functools.partial(kernel, n_slab, n_dom), out_shape=(shape...  55.6 us
    unnamed x4, local copies, waits for them, and re-layouts  1.89 us

profile of v1, /device:TPU:14, one launch (start us, length us, event | category | flops | bytes accessed | tf_op | source)
XLA Modules:
  0.0 59.5 jit_solution(10660510099231915745)
XLA Ops:
  1.9 55.6 %shard_map.122 = (f32[3,1,1,512]{3,2,1,0:T(1,128)}, f32[3,1,1,512]{3,2,1,0:T(1,128)}) custom-call(f32[3,1,1,512]{3,2,1,0:T(1,128)} %coords_ref.1, f32[3,1,1,512]{3,2,1,0:T(1,128)} %velocity_ref.1, f32[1,1,512]{2,1,0:T(1,128)} %charge_ref.1, f32[1,1,512]{2,1,0:T(1,128)} %mass_ref.1, s32[1,1,64]{2,1,0:T(1,128)} %block_ref.1, s32[1,1,64,128]{3,2,1,0:T(8,128)} %atoms_ref.1, ...), custom_call_target="tpu_custom_call" | custom-call | tf_op jit(solution)/shard_map/pallas_call | solution.py:338
  57.6 0.0 copy-start
  57.6 1.3 %copy.17 = f32[3,1,1,512]{3,2,1,0:T(1,128)} copy(f32[3,1,1,512]{3,2,1,0:T(1,128)} %get-tuple-element.4) | data formatting | bytes 12288
  58.9 0.0 copy-done
  58.9 0.6 copy.18
Async XLA Ops:
  57.6 1.3 %copy-start = (f32[3,1,1,512]{3,2,1,0:T(1,128)S(1)}, f32[3,1,1,512]{3,2,1,0:T(1,128)}, u32[]{:S(2)}) copy-start(f32[3,1,1,512]{3,2,1,0:T(1,128)} %get-tuple-element.5) | copy-start | bytes 18436

commit v2 on v1

v2 whole, which is shorter than its diff:
```python
import functools

import jax
import jax.numpy as jnp
from jax import lax
from jax.experimental import pallas as pl
from jax.experimental.pallas import tpu as pltpu
from jax.sharding import PartitionSpec as P

TILE = 128
GROUP = 8

time_step = 0.1
cutoff_sq = 16.0
force_scale = 4.0
length_floor = 0.25

MESH = pl.DeviceIdType.MESH
f32, bf16, i32 = jnp.float32, jnp.bfloat16, jnp.int32

FOURTH = 3
DEPTH = 80
TWO_STEPS = ((0, 0), (1, 1), (2, 2), (3, 3), (0, 2), (0, 3), (1, 2), (1, 3))


def parts3(a):
    high = a.astype(bf16).astype(f32)
    rest = a - high
    mid = rest.astype(bf16).astype(f32)
    low = (rest - mid).astype(bf16).astype(f32)
    return high, mid, low


def lanes(table, index):
    return jnp.take_along_axis(table, index, axis=1, mode="promise_in_bounds")


def row_ids():
    return lax.broadcasted_iota(i32, (8, TILE), 0)


def packed(low, high):
    return jnp.where(row_ids() < 4, low, pltpu.roll(high, 4, 0))


def pack_field(field, halves=2):
    parts = [field[:, g * TILE : (g + 1) * TILE] for g in range(2 * halves)]
    return [packed(a, b) for a, b in zip(parts[::2], parts[1::2])]


def half(picked, group):
    return jnp.where((group & 1) == 1, pltpu.roll(picked, 4, 0), picked)


def from_packed(tables, index):
    low, group = index & (TILE - 1), index >> 7
    picked = lanes(tables[0], low)
    for k in range(1, len(tables)):
        picked = jnp.where((group >> 1) == k, lanes(tables[k], low), picked)
    return half(picked, group)


def spread_row(row):
    return jnp.broadcast_to(row, (8, TILE))


def direction(first, second, mask):
    offset = jnp.where(row_ids() < 3, first - second, 0.0)
    squared = jnp.sum(offset * offset, axis=0, keepdims=True)
    masses = (first + second)[FOURTH : FOURTH + 1, :]
    return offset * (lax.rsqrt(squared + length_floor) * lax.rsqrt(masses) * mask)


def project(scaled_dir, first, second):
    return jnp.sum(scaled_dir * (first - second), axis=0, keepdims=True)


def marks(index, atom_ids):
    return jnp.where(jnp.transpose(index.astype(f32))[:, 0:1] == atom_ids, 1.0, 0.0)


class Domain:
    def __init__(self, bonds, slots, far_slots, own_geo, far_geo, bond_inc, cross_inc):
        self.bond_inc, self.cross_inc = bond_inc, cross_inc
        atom_ids = lax.broadcasted_iota(i32, (TILE, bond_inc.shape[1]), 1).astype(f32)
        self.bond_ends = []
        for g in range(2):
            ends = [spread_row(bonds[2 * e + g : 2 * e + g + 1, :]) for e in range(2)]
            self.bond_ends.append(ends)
            bond_inc[g * TILE : (g + 1) * TILE, :] = (
                marks(ends[0], atom_ids) - marks(ends[1], atom_ids)
            ).astype(bf16)
        self.sides = spread_row(slots[2:3, :])
        self.cross_own, self.cross_far, masks = [], [], []
        for n, table in enumerate([slots] + far_slots):
            mine, theirs = (0, 1) if n == 0 else (1, 0)
            self.cross_own.append(spread_row(table[mine : mine + 1, :]))
            self.cross_far.append(spread_row(table[theirs : theirs + 1, :]))
            code = table[2:3, :]
            alive = code < 4 if n == 0 else code == ((n - 1) ^ 1)
            masks.append(jnp.where(alive, 1.0, 0.0))
            cross_inc[n * TILE : (n + 1) * TILE, :] = marks(
                self.cross_own[-1], atom_ids[:, : 2 * TILE]
            ).astype(bf16)
        ones = jnp.ones((1, TILE), f32)
        self.dirs = [
            direction(a, b, m)
            for (a, b), m in zip(
                self.bond_fields(own_geo) + self.cross_fields(own_geo, far_geo), [ones, ones] + masks
            )
        ]

    def bond_fields(self, own):
        return [(from_packed(own, a), from_packed(own, b)) for a, b in self.bond_ends]

    def cross_fields(self, own, far):
        here = [from_packed(own[:1], c) for c in self.cross_own]
        low, group = self.cross_far[0] & (TILE - 1), self.cross_far[0] >> 7
        picked = lanes(far[0], low)
        for k in range(1, 4):
            picked = jnp.where(self.sides == k, lanes(far[k], low), picked)
        there = [half(picked, group)] + [from_packed([far[k]], self.cross_far[k + 1]) for k in range(4)]
        return list(zip(here, there))

    def bond_changes(self, own):
        return [project(d, a, b) for d, (a, b) in zip(self.dirs[:2], self.bond_fields(own))]

    def cross_changes(self, own, far):
        return [project(d, a, b) for d, (a, b) in zip(self.dirs[2:], self.cross_fields(own, far))]

    def changes(self, own, far):
        return self.bond_changes(own) + self.cross_changes(own, far)

    def spread(self, values):
        pushed = jnp.concatenate([d * v for d, v in zip(self.dirs, values)], axis=1)
        high = pushed.astype(bf16).astype(f32)
        pushed = jnp.concatenate([high, pushed - high], axis=0).astype(bf16)
        bonds = jnp.dot(pushed[:, : 2 * TILE], self.bond_inc[...], preferred_element_type=f32)
        cross = jnp.dot(pushed[:, 2 * TILE :], self.cross_inc[...], preferred_element_type=f32)
        total = bonds[:, : 2 * TILE] + cross
        if bonds.shape[1] > 2 * TILE:
            total = jnp.concatenate([total, bonds[:, 2 * TILE :]], axis=1)
        return total[:8] + total[8:]


def kernel(
    n_slab,
    n_dom,
    coords_hbm,
    velocity_hbm,
    charge_hbm,
    mass_hbm,
    block_hbm,
    atoms_hbm,
    live_hbm,
    bond_hbm,
    cross_hbm,
    side_hbm,
    cross_count_hbm,
    moved_ref,
    velocity_half_ref,
    correction_ref,
    coords_ref,
    velocity_ref,
    charge_ref,
    mass_ref,
    block_ref,
    atoms_ref,
    live_ref,
    bond_ref,
    cross_ref,
    side_ref,
    cross_count_ref,
    load_sem,
    own_ref,
    speed_ref,
    rim_ref,
    inner_ref,
    rims_ref,
    index_ref,
    indices_ref,
    geo2_ref,
    slots2_ref,
    near_ref,
    bond_inc_ref,
    ghost_bond_inc_ref,
    cross_inc_ref,
    field_ref,
    fields_ref,
    fields2_ref,
    rim_send,
    rim_recv,
    index_send,
    index_recv,
    geo2_send,
    geo2_recv,
    slots2_send,
    slots2_recv,
    field_send,
    field_recv,
    field2_send,
    field2_recv,
):
    slab, dom = lax.axis_index("slab"), lax.axis_index("dom")
    width = max(2, n_dom // 8)
    strides = (1, -1, width, -width)

    def holder(stride):
        return slab, lax.rem(dom + 2 * n_dom - stride, n_dom)

    in_slab = [holder(s) for s in strides]
    across = [(lax.rem(slab + n_slab + s, n_slab), dom) for s in (1, -1)]
    beyond = [holder(strides[a] + strides[b]) for a, b in TWO_STEPS]
    targets = in_slab + across

    barrier = pltpu.get_barrier_semaphore()
    for target in targets:
        pl.semaphore_signal(barrier, inc=1, device_id=target, device_id_type=MESH)

    loads = [
        pltpu.make_async_copy(src, dst, load_sem.at[n])
        for n, (src, dst) in enumerate(
            (
                (coords_hbm, coords_ref),
                (charge_hbm, charge_ref),
                (mass_hbm, mass_ref),
                (cross_hbm, cross_ref),
                (side_hbm, side_ref),
                (cross_count_hbm, cross_count_ref),
                (bond_hbm, bond_ref),
                (velocity_hbm, velocity_ref),
                (block_hbm, block_ref),
                (live_hbm, live_ref),
                (atoms_hbm, atoms_ref),
            )
        )
    ]
    for load in loads:
        load.start()
    for load in loads[:7]:
        load.wait()

    for c in range(3):
        own_ref[c : c + 1, :] = coords_ref[c, 0]
        own_ref[4 + c : 5 + c, :] = coords_ref[c, 0]
    own_ref[3:4, :] = mass_ref[0]
    own_ref[7:8, :] = charge_ref[0]
    own = own_ref[...]
    rows = lax.broadcasted_iota(i32, own.shape, 0)
    parts = [own[:, g * TILE : (g + 1) * TILE] for g in range(4)]
    geo = [packed(parts[0], parts[1]), packed(parts[2], parts[3])]
    pair_tables = [jnp.where(row_ids() < 4, pltpu.roll(p, 4, 0), p) for p in parts]
    for g in range(2):
        rim_ref[g] = pair_tables[g]
        rim_ref[2 + g] = geo[g]
        inner_ref[g] = pair_tables[2 + g]
    index_ref[...] = jnp.zeros_like(index_ref)
    index_ref[0:1, :] = cross_ref[0, 0]
    index_ref[1:2, :] = cross_ref[1, 0]
    slot_ids = lax.broadcasted_iota(i32, (1, TILE), 1)
    index_ref[2:3, :] = jnp.where(slot_ids < cross_count_ref[0, 0], side_ref[0], 8)
    for e in range(2):
        for g in range(2):
            row = 8 + 2 * e + g
            index_ref[row : row + 1, :] = bond_ref[e, 0][:, g * TILE : (g + 1) * TILE]

    copies = []

    def send(src, dst, sent, landed, target):
        copy = pltpu.make_async_remote_copy(
            src_ref=src, dst_ref=dst, send_sem=sent, recv_sem=landed, device_id=target, device_id_type=MESH
        )
        copy.start()
        copies.append(copy)
        return copy

    pl.semaphore_wait(barrier, len(targets))
    rims = []
    for n, target in enumerate(targets):
        size = 4 if n < 4 else 2
        rims.append(send(rim_ref.at[pl.ds(0, size)], rims_ref.at[n, pl.ds(0, size)], rim_send.at[n], rim_recv.at[n], target))
    indices = [
        send(index_ref, indices_ref.at[n], index_send.at[n], index_recv.at[n], target)
        for n, target in enumerate(in_slab)
    ]

    norm = own[0:1, :] * own[0:1, :] + own[1:2, :] * own[1:2, :] + own[2:3, :] * own[2:3, :]
    zeros = jnp.zeros_like(own)
    distance = parts3(jnp.where(rows < 3, -2.0 * own, 0.0))
    charges = parts3(jnp.where(rows == 3, force_scale * pltpu.roll(own, 4, 0), 0.0))
    norms = parts3(norm + 1.0)
    for which in range(2):
        constant = jnp.where(rows == 4 * which, 1.0, 0.0)
        tails = [[jnp.where(rows == FOURTH, k, constant) for k in norms] + [zeros], [zeros] * 4]
        for at, ((h, m, l), tail) in enumerate(zip((distance, charges), tails)):
            pieces = [h, m, l, h, m, h]
            if which:
                pieces = [pltpu.roll(p, 4, 0) for p in pieces]
            near = jnp.transpose(jnp.concatenate(pieces + tail, axis=0)).astype(bf16)
            for b in range(4):
                near_ref[which, b, at * TILE : (at + 1) * TILE, :] = near[b * TILE : (b + 1) * TILE, :]

    for copy in indices:
        copy.wait_recv()
    for copy in rims:
        copy.wait_recv()
    geo2, slots2 = [], []
    for n, target in enumerate(beyond):
        geo2.append(send(rim_ref.at[2], geo2_ref.at[n], geo2_send.at[n], geo2_recv.at[n], target))
        slots2.append(send(index_ref.at[pl.ds(0, 8)], slots2_ref.at[n], slots2_send.at[n], slots2_recv.at[n], target))

    for load in loads[7:]:
        load.wait()

    def gather(group):
        index = atoms_ref[0, 0, pl.ds(pl.multiple_of(group * GROUP, GROUP), GROUP), :]
        fars = []
        tables = [rim_ref[0], rim_ref[1], inner_ref[0], inner_ref[1]]
        tables += [rims_ref[n, g] for n in range(6) for g in range(2)]
        ids = row_ids()
        for r in range(GROUP // 2):
            entry = jnp.where(ids < 4, spread_row(index[2 * r : 2 * r + 1, :]), spread_row(index[2 * r + 1 : 2 * r + 2, :]))
            low = entry & (TILE - 1)
            found = [lanes(t, low) for t in tables]
            for bit in range(4):
                upper = (entry & (TILE << bit)) != 0
                found = [jnp.where(upper, b, a) for a, b in zip(found[::2], found[1::2])]
            found = found[0]
            h, m, l = parts3(found)
            fourth = (ids & 3) == FOURTH
            square = jnp.where(fourth, 0.0, found * found)
            square = square + pltpu.roll(square, 7, 0) + pltpu.roll(square, 6, 0)
            squares = [jnp.where(ids == FOURTH, 1.0, s) for s in parts3(square)]
            far = jnp.concatenate([h, h, h, m, m, l] + squares + [jnp.zeros_like(h)], axis=0).astype(bf16)
            far2 = jnp.concatenate([jnp.where(fourth, 1.0, h), jnp.where(fourth, 0.0, m)], axis=0).astype(bf16)
            fars += [far, far2]
        return tuple(fars)

    n_groups = atoms_ref.shape[2] // GROUP

    def pairs(group, carry):
        totals, fars = list(carry[:8]), carry[8:]
        for r in range(GROUP // 2):
            far, far2 = fars[2 * r : 2 * r + 2]
            for which in range(2):
                tile = group * GROUP + 2 * r + which
                block = block_ref[0, 0, tile]
                both = jnp.dot(near_ref[which, block], far, preferred_element_type=f32)
                dist, charge = both[:TILE], both[TILE:]
                inverse = 1.0 / dist
                switch = jnp.maximum((1.0 + 1.0 / cutoff_sq) - dist * (1.0 / cutoff_sq), 0.0)
                edge = inverse * switch
                strength = (2.0 * force_scale * inverse - charge) * (edge * edge)
                high = strength.astype(bf16)
                rest = (strength - high.astype(f32)).astype(bf16)
                summed = lax.dot_general(
                    far2,
                    jnp.concatenate([high, rest], axis=0),
                    (((1,), (1,)), ((), ())),
                    preferred_element_type=f32,
                )
                summed = summed[:, :TILE] + summed[:, TILE:]
                summed = summed[:8] + summed[8:]
                alive = jnp.where(tile < live_ref[0, 0], 1, 0)
                for b in range(4):
                    weight = jnp.where(block == b, alive, 0).astype(f32)
                    totals[4 * which + b] = totals[4 * which + b] + summed * weight
        return tuple(totals) + gather(lax.rem(group + 1, n_groups))

    totals = lax.fori_loop(0, n_groups, pairs, tuple(jnp.zeros((8, TILE), f32) for _ in range(8)) + gather(0))[:8]
    totals = [packed_sum(a, b) for a, b in zip(totals[:4], totals[4:])]
    totals = jnp.concatenate(totals, axis=1)
    speed_ref[...] = jnp.zeros_like(speed_ref)
    for c in range(3):
        speed_ref[c : c + 1, :] = velocity_ref[c, 0]
    mass = own[3:4, :]
    force = jnp.where(rows < 3, own * totals[FOURTH : FOURTH + 1, :] - totals, 0.0)
    velocity_half = speed_ref[...] + time_step * force * mass
    displace = time_step * velocity_half
    moved = own + displace

    def exchange(step, tables):
        for g, table in enumerate(tables):
            field_ref[step, g] = table
        size = len(tables)
        sent = [
            send(
                field_ref.at[step, pl.ds(0, size)],
                fields_ref.at[step, n, pl.ds(0, size)],
                field_send.at[step, n],
                field_recv.at[step, n],
                target,
            )
            for n, target in enumerate(in_slab)
        ]
        if size == 2:
            sent += [
                send(field_ref.at[step, 0], fields2_ref.at[step, n], field2_send.at[step, n], field2_recv.at[step, n], target)
                for n, target in enumerate(beyond)
            ]
        return sent

    def arrive(sent):
        for copy in sent:
            copy.wait_recv()

    def around(n, mine, near_by, two_steps):
        found = []
        for k in range(4):
            pair = (n, k) if (n, k) in TWO_STEPS else (k, n)
            found.append(mine if k == n ^ 1 else two_steps[TWO_STEPS.index(pair)])
        return found

    displaced = pack_field(displace)
    sent = exchange(0, displaced)

    own_index = index_ref[...]
    near_index = [indices_ref[n] for n in range(4)]
    near_geo = [[rims_ref[n, 2], rims_ref[n, 3]] for n in range(4)]
    here = Domain(
        own_index[8:12, :],
        own_index[0:8, :],
        [i[0:8, :] for i in near_index],
        geo,
        [g[0] for g in near_geo],
        bond_inc_ref,
        cross_inc_ref.at[4],
    )
    arrive(geo2 + slots2)
    far_index = [slots2_ref[n] for n in range(8)]
    far_geo = [geo2_ref[n] for n in range(8)]
    ghosts, masses = [], []
    for n in range(4):
        ghosts.append(
            Domain(
                near_index[n][8:12, :],
                near_index[n][0:8, :],
                around(n, own_index[0:8, :], near_index, far_index),
                near_geo[n],
                around(n, geo[0], near_geo, far_geo),
                ghost_bond_inc_ref.at[n],
                cross_inc_ref.at[n],
            )
        )
        first = near_geo[n][0]
        masses.append(jnp.concatenate([first[FOURTH : FOURTH + 1, :], first[4 + FOURTH :, :]], axis=1))

    def ghost_changes(mine, step):
        by = [[fields_ref[step, n, g] for g in range(2)] for n in range(4)]
        two = [fields2_ref[step, n] for n in range(8)]
        return [ghosts[n].changes(by[n], around(n, mine[0], by, two)) for n in range(4)]

    def minus(a, b):
        return [x - y for x, y in zip(a, b)]

    def far_spread(values):
        return [pack_field(g.spread(v) * m, 1)[0] for g, v, m in zip(ghosts, values, masses)]

    local = here.bond_changes(displaced)
    arrive(sent)
    start = local + here.cross_changes(displaced, [fields_ref[0, n, 0] for n in range(4)])
    ghost_start = ghost_changes(displaced, 0)
    field1 = here.spread(start) * mass
    far = far_spread(ghost_start)
    first = minus(start, here.changes(pack_field(field1), far))
    field2 = field1 + here.spread(first) * mass
    both = pack_field(field2)
    sent = exchange(1, both)
    local = here.bond_changes(both)
    arrive(sent)
    second = minus(start, local + here.cross_changes(both, [fields_ref[1, n, 0] for n in range(4)]))
    ghost_second = [minus(a, b) for a, b in zip(ghost_start, ghost_changes(both, 1))]
    field3 = here.spread(second) * mass
    third = minus(second, here.changes(pack_field(field3), far_spread(ghost_second)))
    field4 = pack_field(here.spread(third) * mass)
    sent = exchange(2, field4[:1])
    local = here.bond_changes(field4)
    before = [a + b + c + 2.0 * d for a, b, c, d in zip(start, first, second, third)]
    arrive(sent)
    last = local + here.cross_changes(field4, [fields_ref[2, n, 0] for n in range(4)])
    correction = here.spread(minus(before, last)) * mass
    for c in range(3):
        moved_ref[c, 0] = moved[c : c + 1, :]
        velocity_half_ref[c, 0] = velocity_half[c : c + 1, :]
        correction_ref[c, 0] = correction[c : c + 1, :]
    for copy in copies:
        copy.wait_send()


def packed_sum(first, second):
    return first + pltpu.roll(second, 4, 0)


def shards(coords, velocity, charge, inv_mass, tile_block, tile_atoms, active_tile_count, bond_atoms, cross_atoms, cross_side, cross_count):
    n_slab, n_dom = lax.axis_size("slab"), lax.axis_size("dom")
    atoms = coords.shape[-1]
    tiles = tile_atoms.shape[2]
    shape = jax.ShapeDtypeStruct(coords.shape, f32)
    dma = pltpu.SemaphoreType.DMA
    moved, velocity_half, correction = pl.pallas_call(
        functools.partial(kernel, n_slab, n_dom),
        out_shape=(shape, shape, shape),
        in_specs=[pl.BlockSpec(memory_space=pl.ANY)] * 11,
        out_specs=(pl.BlockSpec(memory_space=pltpu.VMEM),) * 3,
        scratch_shapes=[
            pltpu.VMEM(coords.shape, f32),
            pltpu.VMEM(velocity.shape, f32),
            pltpu.VMEM(charge.shape, f32),
            pltpu.VMEM(inv_mass.shape, f32),
            pltpu.SMEM(tile_block.shape, i32),
            pltpu.VMEM(tile_atoms.shape, i32),
            pltpu.SMEM(active_tile_count.shape, i32),
            pltpu.VMEM(bond_atoms.shape, i32),
            pltpu.VMEM(cross_atoms.shape, i32),
            pltpu.VMEM(cross_side.shape, i32),
            pltpu.SMEM(cross_count.shape, i32),
            dma((11,)),
            pltpu.VMEM((8, atoms), f32),
            pltpu.VMEM((8, atoms), f32),
            pltpu.VMEM((4, 8, TILE), f32),
            pltpu.VMEM((2, 8, TILE), f32),
            pltpu.VMEM((6, 4, 8, TILE), f32),
            pltpu.VMEM((16, TILE), i32),
            pltpu.VMEM((4, 16, TILE), i32),
            pltpu.VMEM((8, 8, TILE), f32),
            pltpu.VMEM((8, 8, TILE), i32),
            pltpu.VMEM((2, 4, 2 * TILE, DEPTH), bf16),
            pltpu.VMEM((2 * TILE, atoms), bf16),
            pltpu.VMEM((4, 2 * TILE, 2 * TILE), bf16),
            pltpu.VMEM((5, 5 * TILE, 2 * TILE), bf16),
            pltpu.VMEM((3, 2, 8, TILE), f32),
            pltpu.VMEM((3, 4, 2, 8, TILE), f32),
            pltpu.VMEM((2, 8, 8, TILE), f32),
            dma((6,)),
            dma((6,)),
            dma((4,)),
            dma((4,)),
            dma((8,)),
            dma((8,)),
            dma((8,)),
            dma((8,)),
            dma((3, 4)),
            dma((3, 4)),
            dma((2, 8)),
            dma((2, 8)),
        ],
        compiler_params=pltpu.CompilerParams(collective_id=0, has_side_effects=True),
    )(coords, velocity, charge, inv_mass, tile_block, tile_atoms, active_tile_count, bond_atoms, cross_atoms, cross_side, cross_count)
    return moved - correction, velocity_half - correction / time_step


def solution(mesh):
    return jax.shard_map(
        shards,
        mesh=mesh,
        in_specs=(
            P(None, "slab", "dom", None),
            P(None, "slab", "dom", None),
            P("slab", "dom", None),
            P("slab", "dom", None),
            P("slab", "dom", None),
            P("slab", "dom", None, None),
            P("slab", "dom"),
            P(None, "slab", "dom", None),
            P(None, "slab", "dom", None),
            P("slab", "dom", None),
            P("slab", "dom"),
        ),
        out_specs=(P(None, "slab", "dom", None), P(None, "slab", "dom", None)),
        check_vma=False,
    )
```

time: 59.7 us -> 50.6 us (0.85)
  Pallas kernels: 55.6 us -> 47 us
  local copies, waits for them, and re-layouts: 1.89 us -> 0 us
  other arithmetic: 0 us -> 1.34 us
    pallas_call x1, Pallas kernels: 55.6 us -> 47 us  [shards(): pl.pallas_call(functools.partial(kernel, n_slab, n_dom), out_shape=(shape...]
    unnamed x4 -> x0, local copies, waits for them, and re-layouts: 1.89 us -> none
    sub x0 -> x1, other arithmetic: none -> 1.34 us  [shards(): return (moved - correction, velocity_half - correction / time_step)]
where the time goes in v2:
time: 50.6 us; the launch traced here: 50.3 us
  Pallas kernels  47 us (93%)
  between operations  1.93 us (4%)
  other arithmetic  1.34 us (3%)
    pallas_call x1, Pallas kernels, shards(): pl.pallas_call(functools.partial(kernel, n_slab, n_dom), out_shape=(shape...  47 us
    sub x1, other arithmetic, shards(): return (moved - correction, velocity_half - correction / time_step)  1.34 us

profile of v2, /device:TPU:14, one launch (start us, length us, event | category | flops | bytes accessed | tf_op | source)
XLA Modules:
  0.0 50.3 jit_solution(3991015575588607603)
XLA Ops:
  1.9 47.0 %shard_map.122 = (f32[3,1,1,512]{3,2,1,0:T(1,128)}, f32[3,1,1,512]{3,2,1,0:T(1,128)}, f32[3,1,1,512]{3,2,1,0:T(1,128)}) custom-call(f32[3,1,1,512]{3,2,1,0:T(1,128)} %coords_hbm.1, f32[3,1,1,512]{3,2,1,0:T(1,128)} %velocity_hbm.1, f32[1,1,512]{2,1,0:T(1,128)} %charge_hbm.1, f32[1,1,512]{2,1,0:T(1,128)} %mass_hbm.1, s32[1,1,64]{2,1,0:T(1,128)} %block_hbm.1, ...), custom_call_target="tpu_custom_call" | custom-call | tf_op jit(solution)/shard_map/pallas_call | solution.py:500
  49.0 1.3 %multiply_subtract_fusion = (f32[3,1,1,512]{3,2,1,0:T(1,128)}, f32[3,1,1,512]{3,2,1,0:T(1,128)}) fusion(f32[3,1,1,512]{3,2,1,0:T(1,128)} %get-tuple-element.7, f32[3,1,1,512]{3,2,1,0:T(1,128)} %get-tuple-element.6, f32[3,1,1,512]{3,2,1,0:T(1,128)} %get-tuple-element.5), kind=kLoop, calls=%fused_computation | loop fusion | flops 4608 | bytes 30720 | tf_op jit(solution)/shard_map/sub | solution.py:549

commit v3 on v2

--- a/solution.py
+++ b/solution.py
@@ -8,7 +8,7 @@
 from jax.sharding import PartitionSpec as P
 
 TILE = 128
-GROUP = 8
+GROUP = 32
 
 time_step = 0.1
 cutoff_sq = 16.0
@@ -152,11 +152,11 @@
     mass_hbm,
     block_hbm,
     atoms_hbm,
-    live_hbm,
+    live_ref,
     bond_hbm,
     cross_hbm,
     side_hbm,
-    cross_count_hbm,
+    cross_count_ref,
     moved_ref,
     velocity_half_ref,
     correction_ref,
@@ -166,11 +166,9 @@
     mass_ref,
     block_ref,
     atoms_ref,
-    live_ref,
     bond_ref,
     cross_ref,
     side_ref,
-    cross_count_ref,
     load_sem,
     own_ref,
     speed_ref,
@@ -226,18 +224,16 @@
                 (mass_hbm, mass_ref),
                 (cross_hbm, cross_ref),
                 (side_hbm, side_ref),
-                (cross_count_hbm, cross_count_ref),
                 (bond_hbm, bond_ref),
                 (velocity_hbm, velocity_ref),
                 (block_hbm, block_ref),
-                (live_hbm, live_ref),
                 (atoms_hbm, atoms_ref),
             )
         )
     ]
     for load in loads:
         load.start()
-    for load in loads[:7]:
+    for load in loads[:6]:
         load.wait()
 
     for c in range(3):
@@ -258,7 +254,7 @@
     index_ref[0:1, :] = cross_ref[0, 0]
     index_ref[1:2, :] = cross_ref[1, 0]
     slot_ids = lax.broadcasted_iota(i32, (1, TILE), 1)
-    index_ref[2:3, :] = jnp.where(slot_ids < cross_count_ref[0, 0], side_ref[0], 8)
+    index_ref[2:3, :] = jnp.where(slot_ids < cross_count_ref[...], side_ref[0], 8)
     for e in range(2):
         for g in range(2):
             row = 8 + 2 * e + g
@@ -286,11 +282,11 @@
 
     norm = own[0:1, :] * own[0:1, :] + own[1:2, :] * own[1:2, :] + own[2:3, :] * own[2:3, :]
     zeros = jnp.zeros_like(own)
-    distance = parts3(jnp.where(rows < 3, -2.0 * own, 0.0))
-    charges = parts3(jnp.where(rows == 3, force_scale * pltpu.roll(own, 4, 0), 0.0))
-    norms = parts3(norm + 1.0)
+    distance = parts3(jnp.where(rows < 3, (-2.0 / cutoff_sq) * own, 0.0))
+    charges = parts3(jnp.where(rows == 3, 2.0 * force_scale * pltpu.roll(own, 4, 0), 0.0))
+    norms = parts3((norm + 1.0) * (1.0 / cutoff_sq))
     for which in range(2):
-        constant = jnp.where(rows == 4 * which, 1.0, 0.0)
+        constant = jnp.where(rows == 4 * which, 1.0 / cutoff_sq, 0.0)
         tails = [[jnp.where(rows == FOURTH, k, constant) for k in norms] + [zeros], [zeros] * 4]
         for at, ((h, m, l), tail) in enumerate(zip((distance, charges), tails)):
             pieces = [h, m, l, h, m, h]
@@ -309,7 +305,7 @@
         geo2.append(send(rim_ref.at[2], geo2_ref.at[n], geo2_send.at[n], geo2_recv.at[n], target))
         slots2.append(send(index_ref.at[pl.ds(0, 8)], slots2_ref.at[n], slots2_send.at[n], slots2_recv.at[n], target))
 
-    for load in loads[7:]:
+    for load in loads[6:]:
         load.wait()
 
     def gather(group):
@@ -337,20 +333,21 @@
         return tuple(fars)
 
     n_groups = atoms_ref.shape[2] // GROUP
+    live = live_ref[...]
 
     def pairs(group, carry):
         totals, fars = list(carry[:8]), carry[8:]
         for r in range(GROUP // 2):
             far, far2 = fars[2 * r : 2 * r + 2]
-            for which in range(2):
+            blocks = [block_ref[0, 0, group * GROUP + 2 * r + which] for which in range(2)]
+            near = jnp.concatenate([near_ref[which, blocks[which]] for which in range(2)], axis=0)
+            both = jnp.dot(near, far, preferred_element_type=f32)
+            for which, block in enumerate(blocks):
                 tile = group * GROUP + 2 * r + which
-                block = block_ref[0, 0, tile]
-                both = jnp.dot(near_ref[which, block], far, preferred_element_type=f32)
-                dist, charge = both[:TILE], both[TILE:]
+                dist, charge = (both[k * TILE : (k + 1) * TILE] for k in (2 * which, 2 * which + 1))
                 inverse = 1.0 / dist
-                switch = jnp.maximum((1.0 + 1.0 / cutoff_sq) - dist * (1.0 / cutoff_sq), 0.0)
-                edge = inverse * switch
-                strength = (2.0 * force_scale * inverse - charge) * (edge * edge)
+                edge = inverse * jnp.maximum((1.0 + 1.0 / cutoff_sq) - dist, 0.0)
+                strength = (inverse - charge) * (edge * edge)
                 high = strength.astype(bf16)
                 rest = (strength - high.astype(f32)).astype(bf16)
                 summed = lax.dot_general(
@@ -361,15 +358,15 @@
                 )
                 summed = summed[:, :TILE] + summed[:, TILE:]
                 summed = summed[:8] + summed[8:]
-                alive = jnp.where(tile < live_ref[0, 0], 1, 0)
+                summed = summed * jnp.where(tile < live, 1.0, 0.0)
                 for b in range(4):
-                    weight = jnp.where(block == b, alive, 0).astype(f32)
+                    weight = jnp.where(block == b, 1, 0).astype(f32)
                     totals[4 * which + b] = totals[4 * which + b] + summed * weight
         return tuple(totals) + gather(lax.rem(group + 1, n_groups))
 
     totals = lax.fori_loop(0, n_groups, pairs, tuple(jnp.zeros((8, TILE), f32) for _ in range(8)) + gather(0))[:8]
     totals = [packed_sum(a, b) for a, b in zip(totals[:4], totals[4:])]
-    totals = jnp.concatenate(totals, axis=1)
+    totals = jnp.concatenate(totals, axis=1) * (1.0 / 512.0)
     speed_ref[...] = jnp.zeros_like(speed_ref)
     for c in range(3):
         speed_ref[c : c + 1, :] = velocity_ref[c, 0]
@@ -497,10 +494,11 @@
     tiles = tile_atoms.shape[2]
     shape = jax.ShapeDtypeStruct(coords.shape, f32)
     dma = pltpu.SemaphoreType.DMA
+    vmem = pl.BlockSpec(memory_space=pltpu.VMEM)
     moved, velocity_half, correction = pl.pallas_call(
         functools.partial(kernel, n_slab, n_dom),
-        out_shape=(shape, shape, shape),
-        in_specs=[pl.BlockSpec(memory_space=pl.ANY)] * 11,
+        out_shape=(pltpu.VMEM(coords.shape, f32),) * 3,
+        in_specs=[vmem if n in (6, 10) else pl.BlockSpec(memory_space=pl.ANY) for n in range(11)],
         out_specs=(pl.BlockSpec(memory_space=pltpu.VMEM),) * 3,
         scratch_shapes=[
             pltpu.VMEM(coords.shape, f32),
@@ -509,12 +507,10 @@
             pltpu.VMEM(inv_mass.shape, f32),
             pltpu.SMEM(tile_block.shape, i32),
             pltpu.VMEM(tile_atoms.shape, i32),
-            pltpu.SMEM(active_tile_count.shape, i32),
             pltpu.VMEM(bond_atoms.shape, i32),
             pltpu.VMEM(cross_atoms.shape, i32),
             pltpu.VMEM(cross_side.shape, i32),
-            pltpu.SMEM(cross_count.shape, i32),
-            dma((11,)),
+            dma((9,)),
             pltpu.VMEM((8, atoms), f32),
             pltpu.VMEM((8, atoms), f32),
             pltpu.VMEM((4, 8, TILE), f32),

time: 50.6 us -> 47.9 us (0.947)
  Pallas kernels: 47 us -> 45.1 us
  other arithmetic: 1.34 us -> 0.61 us
    pallas_call x1, Pallas kernels: 47 us -> 45.1 us  [shards(): pl.pallas_call(functools.partial(kernel, n_slab, n_dom), out_shape=(pltpu...]
    sub x1, other arithmetic: 1.34 us -> 0.61 us  [shards(): return (moved - correction, velocity_half - correction / time_step)]
where the time goes in v3:
time: 47.9 us; the launch traced here: 47.6 us
  Pallas kernels  45.1 us (94%)
  between operations  1.93 us (4%)
  other arithmetic  0.61 us (1%)
    pallas_call x1, Pallas kernels, shards(): pl.pallas_call(functools.partial(kernel, n_slab, n_dom), out_shape=(pltpu...  45.1 us

profile of v3, /device:TPU:14, one launch (start us, length us, event | category | flops | bytes accessed | tf_op | source)
XLA Modules:
  0.0 47.6 jit_solution(1147285437793985817)
XLA Ops:
  1.9 45.1 %shard_map.122 = (f32[3,1,1,512]{3,2,1,0:T(1,128)S(1)}, f32[3,1,1,512]{3,2,1,0:T(1,128)S(1)}, f32[3,1,1,512]{3,2,1,0:T(1,128)S(1)}) custom-call(f32[3,1,1,512]{3,2,1,0:T(1,128)} %coords_hbm.1, f32[3,1,1,512]{3,2,1,0:T(1,128)} %velocity_hbm.1, f32[1,1,512]{2,1,0:T(1,128)} %charge_hbm.1, f32[1,1,512]{2,1,0:T(1,128)} %mass_hbm.1, s32[1,1,64]{2,1,0:T(1,128)} %block_hbm.1, ...), custom_call_target="tpu_custom_call" | custom-call | tf_op jit(solution)/shard_map/pallas_call | solution.py:498
  47.0 0.6 %multiply_subtract_fusion = (f32[3,1,1,512]{3,2,1,0:T(1,128)}, f32[3,1,1,512]{3,2,1,0:T(1,128)}) fusion(f32[3,1,1,512]{3,2,1,0:T(1,128)S(1)} %get-tuple-element.7, f32[3,1,1,512]{3,2,1,0:T(1,128)S(1)} %get-tuple-element.6, f32[3,1,1,512]{3,2,1,0:T(1,128)S(1)} %get-tuple-element.5), kind=kLoop, calls=%fused_computation | loop fusion | flops 4608 | bytes 30720 | tf_op jit(solution)/shard_map/sub | solution.py:545

commit v4 on v3

--- a/solution.py
+++ b/solution.py
@@ -8,7 +8,6 @@
 from jax.sharding import PartitionSpec as P
 
 TILE = 128
-GROUP = 32
 
 time_step = 0.1
 cutoff_sq = 16.0
@@ -308,13 +307,15 @@
     for load in loads[6:]:
         load.wait()
 
-    def gather(group):
-        index = atoms_ref[0, 0, pl.ds(pl.multiple_of(group * GROUP, GROUP), GROUP), :]
+    n_tiles = atoms_ref.shape[2]
+
+    def gather():
+        index = atoms_ref[0, 0]
         fars = []
         tables = [rim_ref[0], rim_ref[1], inner_ref[0], inner_ref[1]]
         tables += [rims_ref[n, g] for n in range(6) for g in range(2)]
         ids = row_ids()
-        for r in range(GROUP // 2):
+        for r in range(n_tiles // 2):
             entry = jnp.where(ids < 4, spread_row(index[2 * r : 2 * r + 1, :]), spread_row(index[2 * r + 1 : 2 * r + 2, :]))
             low = entry & (TILE - 1)
             found = [lanes(t, low) for t in tables]
@@ -332,18 +333,17 @@
             fars += [far, far2]
         return tuple(fars)
 
-    n_groups = atoms_ref.shape[2] // GROUP
     live = live_ref[...]
 
-    def pairs(group, carry):
-        totals, fars = list(carry[:8]), carry[8:]
-        for r in range(GROUP // 2):
+    def pairs(fars):
+        totals = [jnp.zeros((8, TILE), f32) for _ in range(8)]
+        for r in range(n_tiles // 2):
             far, far2 = fars[2 * r : 2 * r + 2]
-            blocks = [block_ref[0, 0, group * GROUP + 2 * r + which] for which in range(2)]
+            blocks = [block_ref[0, 0, 2 * r + which] for which in range(2)]
             near = jnp.concatenate([near_ref[which, blocks[which]] for which in range(2)], axis=0)
             both = jnp.dot(near, far, preferred_element_type=f32)
             for which, block in enumerate(blocks):
-                tile = group * GROUP + 2 * r + which
+                tile = 2 * r + which
                 dist, charge = (both[k * TILE : (k + 1) * TILE] for k in (2 * which, 2 * which + 1))
                 inverse = 1.0 / dist
                 edge = inverse * jnp.maximum((1.0 + 1.0 / cutoff_sq) - dist, 0.0)
@@ -362,9 +362,9 @@
                 for b in range(4):
                     weight = jnp.where(block == b, 1, 0).astype(f32)
                     totals[4 * which + b] = totals[4 * which + b] + summed * weight
-        return tuple(totals) + gather(lax.rem(group + 1, n_groups))
-
-    totals = lax.fori_loop(0, n_groups, pairs, tuple(jnp.zeros((8, TILE), f32) for _ in range(8)) + gather(0))[:8]
+        return totals
+
+    totals = pairs(gather())
     totals = [packed_sum(a, b) for a, b in zip(totals[:4], totals[4:])]
     totals = jnp.concatenate(totals, axis=1) * (1.0 / 512.0)
     speed_ref[...] = jnp.zeros_like(speed_ref)

time: 47.9 us -> 47.3 us (0.987)
  Pallas kernels: 45.1 us -> 44.5 us
    pallas_call x1, Pallas kernels: 45.1 us -> 44.5 us  [shards(): pl.pallas_call(functools.partial(kernel, n_slab, n_dom), out_shape=(pltpu...]
where the time goes in v4:
time: 47.3 us; the launch traced here: 47.1 us
  Pallas kernels  44.5 us (94%)
  between operations  1.93 us (4%)
  other arithmetic  0.61 us (1%)
    pallas_call x1, Pallas kernels, shards(): pl.pallas_call(functools.partial(kernel, n_slab, n_dom), out_shape=(pltpu...  44.5 us

profile of v4, /device:TPU:14, one launch (start us, length us, event | category | flops | bytes accessed | tf_op | source)
XLA Modules:
  0.0 47.1 jit_solution(11365210785179210675)
XLA Ops:
  1.9 44.5 %shard_map.122 = (f32[3,1,1,512]{3,2,1,0:T(1,128)S(1)}, f32[3,1,1,512]{3,2,1,0:T(1,128)S(1)}, f32[3,1,1,512]{3,2,1,0:T(1,128)S(1)}) custom-call(f32[3,1,1,512]{3,2,1,0:T(1,128)} %coords_hbm.1, f32[3,1,1,512]{3,2,1,0:T(1,128)} %velocity_hbm.1, f32[1,1,512]{2,1,0:T(1,128)} %charge_hbm.1, f32[1,1,512]{2,1,0:T(1,128)} %mass_hbm.1, s32[1,1,64]{2,1,0:T(1,128)} %block_hbm.1, ...), custom_call_target="tpu_custom_call" | custom-call | tf_op jit(solution)/shard_map/pallas_call | solution.py:498
  46.5 0.6 %multiply_subtract_fusion = (f32[3,1,1,512]{3,2,1,0:T(1,128)}, f32[3,1,1,512]{3,2,1,0:T(1,128)}) fusion(f32[3,1,1,512]{3,2,1,0:T(1,128)S(1)} %get-tuple-element.7, f32[3,1,1,512]{3,2,1,0:T(1,128)S(1)} %get-tuple-element.6, f32[3,1,1,512]{3,2,1,0:T(1,128)S(1)} %get-tuple-element.5), kind=kLoop, calls=%fused_computation | loop fusion | flops 4608 | bytes 30720 | tf_op jit(solution)/shard_map/sub | solution.py:545

commit v5 on v4

--- a/solution.py
+++ b/solution.py
@@ -272,8 +272,12 @@
     pl.semaphore_wait(barrier, len(targets))
     rims = []
     for n, target in enumerate(targets):
-        size = 4 if n < 4 else 2
+        size = 2
         rims.append(send(rim_ref.at[pl.ds(0, size)], rims_ref.at[n, pl.ds(0, size)], rim_send.at[n], rim_recv.at[n], target))
+    shells = [
+        send(rim_ref.at[pl.ds(2, 2)], rims_ref.at[n, pl.ds(2, 2)], rim_send.at[6 + n], rim_recv.at[6 + n], target)
+        for n, target in enumerate(in_slab)
+    ]
     indices = [
         send(index_ref, indices_ref.at[n], index_send.at[n], index_recv.at[n], target)
         for n, target in enumerate(in_slab)
@@ -295,8 +299,6 @@
             for b in range(4):
                 near_ref[which, b, at * TILE : (at + 1) * TILE, :] = near[b * TILE : (b + 1) * TILE, :]
 
-    for copy in indices:
-        copy.wait_recv()
     for copy in rims:
         copy.wait_recv()
     geo2, slots2 = [], []
@@ -411,6 +413,7 @@
     displaced = pack_field(displace)
     sent = exchange(0, displaced)
 
+    arrive(shells + indices)
     own_index = index_ref[...]
     near_index = [indices_ref[n] for n in range(4)]
     near_geo = [[rims_ref[n, 2], rims_ref[n, 3]] for n in range(4)]
@@ -527,8 +530,8 @@
             pltpu.VMEM((3, 2, 8, TILE), f32),
             pltpu.VMEM((3, 4, 2, 8, TILE), f32),
             pltpu.VMEM((2, 8, 8, TILE), f32),
-            dma((6,)),
-            dma((6,)),
+            dma((10,)),
+            dma((10,)),
             dma((4,)),
             dma((4,)),
             dma((8,)),

time: 47.3 us -> 47.1 us (level)
  no operation moved by 1% of the time
where the time goes in v5:
time: 47.1 us; the launch traced here: 46.8 us
  Pallas kernels  44.3 us (94%)
  between operations  1.93 us (4%)
  other arithmetic  0.61 us (1%)
    pallas_call x1, Pallas kernels, shards(): pl.pallas_call(functools.partial(kernel, n_slab, n_dom), out_shape=(pltpu...  44.3 us

profile of v5, /device:TPU:14, one launch (start us, length us, event | category | flops | bytes accessed | tf_op | source)
XLA Modules:
  0.0 46.8 jit_solution(10255560148695914523)
XLA Ops:
  1.9 44.3 %shard_map.122 = (f32[3,1,1,512]{3,2,1,0:T(1,128)S(1)}, f32[3,1,1,512]{3,2,1,0:T(1,128)S(1)}, f32[3,1,1,512]{3,2,1,0:T(1,128)S(1)}) custom-call(f32[3,1,1,512]{3,2,1,0:T(1,128)} %coords_hbm.1, f32[3,1,1,512]{3,2,1,0:T(1,128)} %velocity_hbm.1, f32[1,1,512]{2,1,0:T(1,128)} %charge_hbm.1, f32[1,1,512]{2,1,0:T(1,128)} %mass_hbm.1, s32[1,1,64]{2,1,0:T(1,128)} %block_hbm.1, ...), custom_call_target="tpu_custom_call" | custom-call | tf_op jit(solution)/shard_map/pallas_call | solution.py:501
  46.2 0.6 %multiply_subtract_fusion = (f32[3,1,1,512]{3,2,1,0:T(1,128)}, f32[3,1,1,512]{3,2,1,0:T(1,128)}) fusion(f32[3,1,1,512]{3,2,1,0:T(1,128)S(1)} %get-tuple-element.7, f32[3,1,1,512]{3,2,1,0:T(1,128)S(1)} %get-tuple-element.6, f32[3,1,1,512]{3,2,1,0:T(1,128)S(1)} %get-tuple-element.5), kind=kLoop, calls=%fused_computation | loop fusion | flops 4608 | bytes 30720 | tf_op jit(solution)/shard_map/sub | solution.py:548
